TPU v7x, 128 devices: a whole 4x4x4 slice. The times are simulated.
128 devices in a mesh: vrow: 8 (over z, y_hi), img: 16 (over x, y_lo, core).
Axes of the slice: x: 4, y: 4 (y_hi: 2, y_lo: 2; y = y_hi * 2 + y_lo), z: 4, core: 2. Of those that a mesh axis runs over, the one named last changes fastest.
Arguments:
- features: bfloat16 [8, 16, 128, 1024], P('vrow', None, 'img'), may hold values from -6 to 6
- weight_h: bfloat16 [64, 64, 3, 3], replicated, may hold values from -0.25 to 0.25
- weight_v: bfloat16 [64, 64, 3, 3], replicated, may hold values from -0.25 to 0.25
- beta_h: float32 [5, 64], replicated, may hold values from 0.2 to 1
- beta_v: float32 [5, 64], replicated, may hold values from 0.2 to 1
- shear_set: int32 [5], replicated, may hold values from -2 to 2
- cotangent: bfloat16 [16, 128, 8192], P('vrow', 'img'), may hold values from -6 to 6
Outputs:
- output: bfloat16 [16, 128, 8192], P('vrow', 'img')
- grad_features: bfloat16 [8, 16, 128, 1024], P('vrow', None, 'img')
- grad_weight_h: float32 [64, 64, 3, 3], replicated
- grad_weight_v: float32 [64, 64, 3, 3], replicated
- grad_beta_h: float32 [5, 64], replicated
- grad_beta_v: float32 [5, 64], replicated
All inputs are finite; a program needn't handle non-finite values.
Results may differ from a plain program's by a relative error of at most 0.0057.
Values may be sent and summed in bfloat16 or wider, within the bound.
No kernel may reach another device: no remote copies, remote signals or barrier semaphores. Data moves between devices by JAX's collectives and lax.ppermute only.
A program may use at most 128 MiB of HBM per device.

v0:
```python
import jax
import jax.numpy as jnp
from jax import lax
from jax.sharding import PartitionSpec as P

SHIFT_MAX = 2


def conv_taps(source, kernel_row):
    return lax.conv_general_dilated(
        source,
        kernel_row,
        (1, 1),
        ((0, 0), (0, 0)),
        dimension_numbers=("NCHW", "OIHW", "NCHW"),
        preferred_element_type=jnp.float32,
    )


def conv_back(grads, kernel_row):
    return lax.conv_general_dilated(
        grads,
        kernel_row,
        (1, 1),
        ((0, 0), (0, 0)),
        dimension_numbers=("NCHW", "IOHW", "NCHW"),
        preferred_element_type=jnp.float32,
    )


def conv_weight(grads, source):
    result = lax.conv_general_dilated(
        source,
        grads,
        (1, 1),
        ((0, 0), (0, 0)),
        dimension_numbers=("CNHW", "IOHW", "NCHW"),
        preferred_element_type=jnp.float32,
    )
    return jnp.transpose(result, (1, 0, 2, 3))


def view_offsets(count):
    return jnp.arange(count, dtype=jnp.int32) - count // 2


def pad_views(field):
    return jnp.pad(field, ((0, 0), (0, 0), (1, 1), (0, 0)))


def window(padded, row_start, col_start, width):
    starts = (jnp.int32(0), jnp.int32(0), jnp.int32(row_start), jnp.asarray(col_start))
    sizes = (padded.shape[0], padded.shape[1], padded.shape[2] - 2, width + 2)
    return lax.dynamic_slice(padded, starts, sizes)


def masked_source(extended, amounts, start, total):
    columns = start + jnp.arange(extended.shape[3], dtype=jnp.int32)
    shifted = columns[None, :] - amounts[:, None]
    inside = (shifted >= 0) & (shifted < total)
    return (extended * inside[None, None].astype(extended.dtype), inside)


def forward_pass(extended, kernel, blend, shear_set, start, total, reach):
    width = extended.shape[3] - 2 * reach
    offsets = view_offsets(extended.shape[2])
    source_local = extended[:, :, :, reach : reach + width]
    branch = jnp.zeros(source_local.shape, jnp.float32)
    saved = []
    for shear_idx in range(shear_set.shape[0]):
        disparity = shear_set[shear_idx]
        amounts = disparity * offsets
        masked, inside = masked_source(extended, amounts, start, total)
        masked_pad = pad_views(masked)
        preact = jnp.zeros(source_local.shape, jnp.float32)
        for tap_row in range(3):
            piece = window(masked_pad, tap_row, reach - 1 + (tap_row - 1) * disparity, width)
            preact = preact + conv_taps(piece, kernel[:, :, tap_row : tap_row + 1, :])
        keep = inside[:, reach : reach + width].astype(jnp.float32)[None, None]
        branch = branch + blend[shear_idx][None, :, None, None] * (keep * jax.nn.silu(preact))
        saved.append((masked_pad, preact, keep, disparity))
    return ((source_local.astype(jnp.float32) + branch).astype(jnp.bfloat16), saved)


def backward_pass(kernel, blend, grads, saved, extend, reach):
    width = grads.shape[3]
    channels = kernel.shape[0]
    kernel_grad = jnp.zeros((channels, channels, 3, 3), jnp.float32)
    blend_rows = []
    dpre_list = []
    for shear_idx in range(len(saved)):
        masked_pad, preact, keep, disparity = saved[shear_idx]
        blend_rows.append(jnp.sum(grads * (keep * jax.nn.silu(preact)), axis=(0, 2, 3)))
        sigma = jax.nn.sigmoid(preact)
        slope = sigma * (1.0 + preact * (1.0 - sigma))
        dpre = (blend[shear_idx][None, :, None, None] * grads * slope * keep).astype(jnp.bfloat16)
        dpre_list.append(dpre)
        pieces = []
        for tap_row in range(3):
            piece = window(masked_pad, tap_row, reach - 1 + (tap_row - 1) * disparity, width)
            pieces.append(conv_weight(dpre, piece))
        kernel_grad = kernel_grad + jnp.concatenate(pieces, axis=2)
    stacked = extend(jnp.stack(dpre_list))
    total = grads
    for shear_idx in range(len(saved)):
        masked_pad, preact, keep, disparity = saved[shear_idx]
        dpre_pad = pad_views(stacked[shear_idx])
        inputs_grad = jnp.zeros(grads.shape, jnp.float32)
        for tap_row in range(3):
            piece = window(dpre_pad, 2 - tap_row, reach - 1 - (tap_row - 1) * disparity, width)
            inputs_grad = inputs_grad + conv_back(piece, kernel[:, :, tap_row : tap_row + 1, ::-1])
        total = total + keep * inputs_grad
    return (total.astype(jnp.bfloat16), kernel_grad, jnp.stack(blend_rows))


def per_device(features, weight_h, weight_v, beta_h, beta_v, shear_set, cotangent):
    reach = SHIFT_MAX + 1
    vrow_count = lax.axis_size("vrow")
    img_count = lax.axis_size("img")
    channels = weight_h.shape[0]
    u_local, y_all, x_local, merged = features.shape
    v_all = merged // channels
    v_local = v_all // vrow_count
    u_all = u_local * vrow_count
    x_all = x_local * img_count
    y_local = y_all // img_count

    def zero_rims(field):
        widths = [(0, 0)] * (field.ndim - 1) + [(reach, reach)]
        return jnp.pad(field, widths)

    lines = lax.all_to_all(features, "img", split_axis=1, concat_axis=2, tiled=True)
    layout = jnp.transpose(
        lines.reshape(u_local, y_local, x_all, v_all, channels), (0, 1, 4, 3, 2)
    ).reshape(u_local * y_local, channels, v_all, x_all)
    extended_h = zero_rims(layout)
    start_h = -reach
    hfeat, saved_h = forward_pass(extended_h, weight_h, beta_h, shear_set, start_h, x_all, reach)
    block = hfeat.reshape(u_local, y_local, channels, v_all, x_all)
    moved = lax.all_to_all(
        lax.all_to_all(block, "vrow", split_axis=3, concat_axis=0, tiled=True),
        "img",
        split_axis=4,
        concat_axis=1,
        tiled=True,
    )
    vert_in = jnp.transpose(moved, (3, 4, 2, 0, 1)).reshape(
        v_local * x_local, channels, u_all, y_all
    )
    vout, saved_v = forward_pass(
        zero_rims(vert_in), weight_v, beta_v, shear_set, -reach, y_all, reach
    )
    output = jnp.transpose(
        vout.reshape(v_local, x_local, channels, u_all, y_all), (0, 1, 3, 4, 2)
    ).reshape(v_local, x_local, u_all * y_all * channels)
    grad_v = (
        jnp.transpose(cotangent.reshape(v_local, x_local, u_all, y_all, channels), (0, 1, 4, 2, 3))
        .reshape(v_local * x_local, channels, u_all, y_all)
        .astype(jnp.float32)
    )
    dvert, raw_weight_v, raw_beta_v = backward_pass(
        weight_v, beta_v, grad_v, saved_v, zero_rims, reach
    )
    back_block = jnp.transpose(
        dvert.reshape(v_local, x_local, channels, u_all, y_all), (3, 4, 2, 0, 1)
    )
    returned = lax.all_to_all(
        lax.all_to_all(back_block, "vrow", split_axis=0, concat_axis=3, tiled=True),
        "img",
        split_axis=1,
        concat_axis=4,
        tiled=True,
    )
    grad_h = returned.reshape(u_local * y_local, channels, v_all, x_all)
    dhor, raw_weight_h, raw_beta_h = backward_pass(
        weight_h, beta_h, grad_h.astype(jnp.float32), saved_h, zero_rims, reach
    )
    dhor_stored = jnp.transpose(
        dhor.reshape(u_local, y_local, channels, v_all, x_all), (0, 1, 4, 3, 2)
    ).reshape(u_local, y_local, x_all, v_all * channels)
    grad_features = lax.all_to_all(dhor_stored, "img", split_axis=2, concat_axis=1, tiled=True)
    raw_weight_h, raw_weight_v, raw_beta_h, raw_beta_v = lax.psum(
        (raw_weight_h, raw_weight_v, raw_beta_h, raw_beta_v), ("vrow", "img")
    )
    factor = float(u_all * v_all * y_all * x_all) ** (-0.5)
    return (
        output,
        grad_features,
        raw_weight_h * factor,
        raw_weight_v * factor,
        raw_beta_h * factor,
        raw_beta_v * factor,
    )


def solution(mesh):
    placed = (P("vrow", None, "img", None), P(), P(), P(), P(), P(), P("vrow", "img", None))
    return jax.shard_map(
        per_device,
        mesh=mesh,
        in_specs=placed,
        out_specs=(P("vrow", "img", None), P("vrow", None, "img", None), P(), P(), P(), P()),
        check_vma=False,
    )
```

profile of v0, /device:TPU:1, one launch (start us, length us, event | category | flops | bytes accessed | tf_op | source)
XLA Modules:
  0.0 720.8 jit_solution(4382883863679388415)
XLA Ops:
  7.2 6.8 all-to-all-start
  38.2 15.4 %broadcast_multiply_fusion.4 = (bf16[1,64,16,134]{1,0,3,2:T(2,128)(2,1)S(1)}, bf16[1,64,16,134]{1,0,3,2:T(2,128)(2,1)S(1)}, bf16[1,64,16,134]{1,0,3,2:T(2,128)(2...) fusion(bf16[16,134]{1,0:T(8,128)(2,1)S(1)} %copy-done.121, bf16[1,64,16,128]{1,0,3,2:T(2,128)(2,1)S(1)} %copy.364, ...), kind=kLoop, calls=%fused_computation.390 | loop fusion | flops 686080 | bytes 1655744 | tf_op jit(solution)/shard_map/mul | solution.py:61
  58.2 2.8 copy.370
  67.7 2.8 copy.384
  79.1 2.7 copy.398
  85.6 3.6 copy.411
  91.2 2.7 copy.412
  97.6 3.7 copy.425
  103.5 2.7 copy.426
  109.8 3.6 pad_dynamic-slice_fusion.39
  113.5 2.8 copy.365
  132.4 6.5 pad_dynamic-slice_fusion.35
  138.8 3.0 copy.393
  154.8 3.1 add_multiply_fusion.3
  159.0 3.7 add_multiply_fusion.2
  164.0 2.6 copy.543
  166.7 6.9 pad_dynamic-slice_fusion.31
  173.5 2.8 copy.421
  200.7 2.7 add_multiply_fusion.1
  206.5 3.8 add_multiply_fusion
  211.6 2.6 copy.545
  216.6 7.4 %all-to-all-start.1 = ((bf16[1,1,64,16,128]{4,2,1,0,3:T(8,128)(2,1)}), bf16[1,1,64,16,128]{4,2,1,0,3:T(8,128)(2,1)S(1)}, u32[]{:S(2)}, u32[]{:S(2)}) async-start(bf16[1,1,64,16,128]{4,2,1,0,3:T(8,128)(2,1)} %copy.435), calls=%async_computation.1 | async-start | bytes 524288 | tf_op jit(solution)/shard_map/all_to_all | solution.py:141
  224.7 7.8 %all-to-all-done.1 = bf16[1,1,64,16,128]{4,2,1,0,3:T(8,128)(2,1)S(1)} async-done(((bf16[1,1,64,16,128]{4,2,1,0,3:T(8,128)(2,1)}), bf16[1,1,64,16,128]{4,2,1,0,3:T(8,128)(2,1)S(1)}, u32[]{:S(2)}, u32[]{:S(2)}) %all-to-all-start.1) | async-done | bytes 262176 | tf_op jit(solution)/shard_map/all_to_all | solution.py:141
  234.4 6.1 all-to-all-start.2
  317.1 4.1 all-to-all-start.3
  321.2 5.7 fusion.86
  332.5 6.3 all-to-all-start.4
  353.9 4.3 fusion.665
  358.2 4.5 fusion.666
  362.7 4.5 fusion.664
  368.5 4.3 fusion.662
  372.8 4.5 fusion.663
  377.4 4.5 fusion.661
  383.1 4.3 fusion.659
  387.5 4.5 fusion.660
  392.0 4.5 fusion.658
  397.8 4.3 fusion.656
  402.1 3.9 fusion.657
  406.0 4.5 fusion.655
  411.8 4.3 fusion.653
  416.1 4.5 fusion.654
  420.7 4.5 fusion.652
  425.2 3.0 fusion.363
  478.9 2.6 copy.551
  481.6 3.1 fusion.301
  485.4 63.5 %all-reduce.24 = (f32[5,64]{1,0:T(8,128)S(1)}, f32[5,64]{1,0:T(8,128)S(1)}) all-reduce(f32[5,64]{1,0:T(8,128)S(1)} %stack.89, f32[5,64]{1,0:T(8,128)S(1)} %copy-done.126), channel_id=1, replica_groups=mesh['vrow'=8,'img'=16] {'vrow','img'}, use_global_device_ids=true, to_apply=%region_7.8 | all-reduce | flops 640 | bytes 5120 | tf_op jit(solution)/shard_map/psum | solution.py:182
  553.8 4.0 all-to-all-start.5
  559.4 150.5 %all-reduce.28.cloned.1.call-done = (f32[64,64,3,3]{0,1,3,2:T(8,128)}, f32[64,64,3,3]{0,1,3,2:T(8,128)}) async-done(((f32[64,64,3,3]{0,1,3,2:T(8,128)}, f32[64,64,3,3]{0,1,3,2:T(8,128)}), (f32[64,64,3,3]{0,1,3,2:T(8,128)}, f32[64,64,3,3]{0,1,3,2:T(8,128)})) %all-reduce.28.cloned.1.call-update) | async-done | bytes 294928 | tf_op jit(solution)/shard_map/psum | solution.py:182
  (645 shorter events, 263.7 us)
Async XLA Ops:
  7.2 29.0 %all-to-all-start = ((bf16[1,16,8,1024]{3,2,0,1:T(8,128)(2,1)}), bf16[1,16,8,1024]{3,2,0,1:T(8,128)(2,1)S(1)}, u32[]{:S(2)}, u32[]{:S(2)}) async-start(bf16[1,16,8,1024]{3,2,0,1:T(8,128)(2,1)} %bitcast.649), calls=%async_computation | async-start | bytes 524288 | tf_op jit(solution)/shard_map/all_to_all | solution.py:132
  53.6 56.2 %copy-start.3 = (bf16[1,64,16,134]{1,0,3,2:T(2,128)(2,1)}, bf16[1,64,16,134]{1,0,3,2:T(2,128)(2,1)S(1)}, u32[]{:S(2)}) copy-start(bf16[1,64,16,134]{1,0,3,2:T(2,128)(2,1)S(1)} %get-tuple-element.100) | copy-start | bytes 823300
  53.6 78.7 %copy-start.5 = (bf16[1,64,16,134]{1,0,3,2:T(2,128)(2,1)}, bf16[1,64,16,134]{1,0,3,2:T(2,128)(2,1)S(1)}, u32[]{:S(2)}) copy-start(bf16[1,64,16,134]{1,0,3,2:T(2,128)(2,1)S(1)} %get-tuple-element.101) | copy-start | bytes 823300
  53.6 78.7 %copy-start.7 = (bf16[1,64,16,134]{1,0,3,2:T(2,128)(2,1)}, bf16[1,64,16,134]{1,0,3,2:T(2,128)(2,1)S(1)}, u32[]{:S(2)}) copy-start(bf16[1,64,16,134]{1,0,3,2:T(2,128)(2,1)S(1)} %get-tuple-element.102) | copy-start | bytes 823300
  132.3 81.9 %copy-start.12 = (f32[16,1,128,64]{2,0,3,1:T(8,128)}, f32[16,1,128,64]{2,0,3,1:T(8,128)S(1)}, u32[]{:S(2)}) copy-start(f32[16,1,128,64]{2,0,3,1:T(8,128)S(1)} %copy.541) | copy-start | bytes 1572868
  159.0 55.2 %copy-start.14 = (f32[16,1,128,64]{2,0,3,1:T(8,128)}, f32[16,1,128,64]{2,0,3,1:T(8,128)S(1)}, u32[]{:S(2)}) copy-start(f32[16,1,128,64]{2,0,3,1:T(8,128)S(1)} %copy.542) | copy-start | bytes 1572868
  206.4 7.8 %copy-start.18 = (f32[16,1,128,64]{2,0,3,1:T(8,128)}, f32[16,1,128,64]{2,0,3,1:T(8,128)S(1)}, u32[]{:S(2)}) copy-start(f32[16,1,128,64]{2,0,3,1:T(8,128)S(1)} %copy.544) | copy-start | bytes 1572868
  214.3 9.6 %copy-start.153 = (f32[5,64]{1,0:T(8,128)S(1)}, f32[5,64]{1,0:T(8,128)}, u32[]{:S(2)}) copy-start(f32[5,64]{1,0:T(8,128)} %param.11) | copy-start | bytes 3844
  214.3 10.2 %copy-start.140 = (pred[8,22]{1,0:T(8,128)(4,1)S(1)}, pred[8,22]{1,0:T(8,128)(4,1)}, u32[]{:S(2)}) copy-start(pred[8,22]{1,0:T(8,128)(4,1)} %get-tuple-element.141) | copy-start | bytes 532
  214.4 10.2 %copy-start.141 = (pred[8,22]{1,0:T(8,128)(4,1)S(1)}, pred[8,22]{1,0:T(8,128)(4,1)}, u32[]{:S(2)}) copy-start(pred[8,22]{1,0:T(8,128)(4,1)} %get-tuple-element.164) | copy-start | bytes 532
  216.6 15.9 %all-to-all-start.1 = ((bf16[1,1,64,16,128]{4,2,1,0,3:T(8,128)(2,1)}), bf16[1,1,64,16,128]{4,2,1,0,3:T(8,128)(2,1)S(1)}, u32[]{:S(2)}, u32[]{:S(2)}) async-start(bf16[1,1,64,16,128]{4,2,1,0,3:T(8,128)(2,1)} %copy.435), calls=%async_computation.1 | async-start | bytes 524288 | tf_op jit(solution)/shard_map/all_to_all | solution.py:141
  224.6 47.6 %copy-start.142 = (f32[64]{0:T(128)}, f32[64]{0:T(128)S(1)}, u32[]{:S(2)}) copy-start(f32[64]{0:T(128)S(1)} %get-tuple-element.126) | copy-start | bytes 772
  233.0 7.6 %copy-start.139 = (pred[8,22]{1,0:T(8,128)(4,1)S(1)}, pred[8,22]{1,0:T(8,128)(4,1)}, u32[]{:S(2)}) copy-start(pred[8,22]{1,0:T(8,128)(4,1)} %get-tuple-element.166) | copy-start | bytes 532
  234.4 20.1 %copy-start.137 = (pred[8,22]{1,0:T(8,128)(4,1)S(1)}, pred[8,22]{1,0:T(8,128)(4,1)}, u32[]{:S(2)}) copy-start(pred[8,22]{1,0:T(8,128)(4,1)} %get-tuple-element.160) | copy-start | bytes 532
  234.4 20.1 %copy-start.138 = (pred[8,22]{1,0:T(8,128)(4,1)S(1)}, pred[8,22]{1,0:T(8,128)(4,1)}, u32[]{:S(2)}) copy-start(pred[8,22]{1,0:T(8,128)(4,1)} %get-tuple-element.162) | copy-start | bytes 532
  234.4 20.2 %copy-start.50 = (f32[16,8,17,64]{3,1,2,0:T(8,128)S(1)}, f32[16,8,17,64]{3,1,2,0:T(8,128)}, u32[]{:S(2)}) copy-start(f32[16,8,17,64]{3,1,2,0:T(8,128)} %get-tuple-element.88) | copy-start | bytes 1671172
  234.4 33.3 %all-to-all-start.2 = ((bf16[16,2,4096]{2,1,0:T(2,128)(2,1)}), bf16[16,2,4096]{2,1,0:T(2,128)(2,1)}, u32[]{:S(2)}, u32[]{:S(2)}) async-start(bf16[16,2,4096]{2,1,0:T(2,128)(2,1)} %reshape.837), calls=%async_computation.2 | async-start | bytes 524288 | tf_op jit(solution)/shard_map/all_to_all | solution.py:140
  315.0 6.2 copy-start.143
  317.1 12.8 %all-to-all-start.3 = ((bf16[8,2,8192]{2,1,0:T(2,128)(2,1)}), bf16[8,2,8192]{2,1,0:T(2,128)(2,1)}, u32[]{:S(2)}, u32[]{:S(2)}) async-start(bf16[8,2,8192]{2,1,0:T(2,128)(2,1)} %reshape.839), calls=%async_computation.3 | async-start | bytes 524288 | tf_op jit(solution)/shard_map/all_to_all | solution.py:168
  321.2 5.8 copy-start.159
  331.3 7.5 %copy-start.160 = (bf16[16,64,8,16]{1,0,3,2:T(8,128)(2,1)S(1)}, bf16[16,64,8,16]{1,0,3,2:T(8,128)(2,1)}, u32[]{:S(2)}) copy-start(bf16[16,64,8,16]{1,0,3,2:T(8,128)(2,1)} %copy-done.158) | copy-start | bytes 786436
  332.5 13.7 %all-to-all-start.4 = ((bf16[16,2,4096]{2,1,0:T(2,128)(2,1)}), bf16[16,2,4096]{2,1,0:T(2,128)(2,1)S(1)}, u32[]{:S(2)}, u32[]{:S(2)}) async-start(bf16[16,2,4096]{2,1,0:T(2,128)(2,1)} %reshape.841), calls=%async_computation.4 | async-start | bytes 524288 | tf_op jit(solution)/shard_map/all_to_all | solution.py:167
  358.2 4.5 copy-start.35
  372.8 4.5 copy-start.32
  377.4 4.5 copy-start.58
  387.5 4.5 copy-start.28
  392.0 4.5 copy-start.57
  406.0 4.5 copy-start.56
  416.1 4.5 copy-start.21
  420.7 4.5 copy-start.49
  477.1 4.5 copy-start.72
  477.1 4.5 copy-start.74
  550.1 7.7 %copy-start.79 = (f32[64,64,1,3]{0,1,3,2:T(8,128)S(1)}, f32[64,64,1,3]{0,1,3,2:T(8,128)}, u32[]{:S(2)}) copy-start(f32[64,64,1,3]{0,1,3,2:T(8,128)} %fusion.665) | copy-start | bytes 147460
  550.1 7.7 %copy-start.80 = (f32[64,64,1,3]{0,1,3,2:T(8,128)S(1)}, f32[64,64,1,3]{0,1,3,2:T(8,128)}, u32[]{:S(2)}) copy-start(f32[64,64,1,3]{0,1,3,2:T(8,128)} %fusion.666) | copy-start | bytes 147460
  550.1 7.7 %copy-start.81 = (f32[64,64,1,3]{0,1,3,2:T(8,128)S(1)}, f32[64,64,1,3]{0,1,3,2:T(8,128)}, u32[]{:S(2)}) copy-start(f32[64,64,1,3]{0,1,3,2:T(8,128)} %fusion.664) | copy-start | bytes 147460
  550.2 7.7 %copy-start.82 = (f32[64,64,1,3]{0,1,3,2:T(8,128)S(1)}, f32[64,64,1,3]{0,1,3,2:T(8,128)}, u32[]{:S(2)}) copy-start(f32[64,64,1,3]{0,1,3,2:T(8,128)} %fusion.662) | copy-start | bytes 147460
  550.2 7.7 %copy-start.83 = (f32[64,64,1,3]{0,1,3,2:T(8,128)S(1)}, f32[64,64,1,3]{0,1,3,2:T(8,128)}, u32[]{:S(2)}) copy-start(f32[64,64,1,3]{0,1,3,2:T(8,128)} %fusion.663) | copy-start | bytes 147460
  550.2 7.7 %copy-start.84 = (f32[64,64,1,3]{0,1,3,2:T(8,128)S(1)}, f32[64,64,1,3]{0,1,3,2:T(8,128)}, u32[]{:S(2)}) copy-start(f32[64,64,1,3]{0,1,3,2:T(8,128)} %fusion.661) | copy-start | bytes 147460
  550.2 7.7 %copy-start.85 = (f32[64,64,1,3]{0,1,3,2:T(8,128)S(1)}, f32[64,64,1,3]{0,1,3,2:T(8,128)}, u32[]{:S(2)}) copy-start(f32[64,64,1,3]{0,1,3,2:T(8,128)} %fusion.659) | copy-start | bytes 147460
  550.2 7.7 %copy-start.86 = (f32[64,64,1,3]{0,1,3,2:T(8,128)S(1)}, f32[64,64,1,3]{0,1,3,2:T(8,128)}, u32[]{:S(2)}) copy-start(f32[64,64,1,3]{0,1,3,2:T(8,128)} %fusion.660) | copy-start | bytes 147460
  550.2 7.7 %copy-start.87 = (f32[64,64,1,3]{0,1,3,2:T(8,128)S(1)}, f32[64,64,1,3]{0,1,3,2:T(8,128)}, u32[]{:S(2)}) copy-start(f32[64,64,1,3]{0,1,3,2:T(8,128)} %fusion.658) | copy-start | bytes 147460
  550.2 7.7 %copy-start.88 = (f32[64,64,1,3]{0,1,3,2:T(8,128)S(1)}, f32[64,64,1,3]{0,1,3,2:T(8,128)}, u32[]{:S(2)}) copy-start(f32[64,64,1,3]{0,1,3,2:T(8,128)} %fusion.656) | copy-start | bytes 147460
  550.2 7.7 %copy-start.89 = (f32[64,64,1,3]{0,1,3,2:T(8,128)S(1)}, f32[64,64,1,3]{0,1,3,2:T(8,128)}, u32[]{:S(2)}) copy-start(f32[64,64,1,3]{0,1,3,2:T(8,128)} %fusion.655) | copy-start | bytes 147460
  550.2 7.7 %copy-start.90 = (f32[64,64,1,3]{0,1,3,2:T(8,128)S(1)}, f32[64,64,1,3]{0,1,3,2:T(8,128)}, u32[]{:S(2)}) copy-start(f32[64,64,1,3]{0,1,3,2:T(8,128)} %fusion.653) | copy-start | bytes 147460
  550.2 7.7 %copy-start.91 = (f32[64,64,1,3]{0,1,3,2:T(8,128)S(1)}, f32[64,64,1,3]{0,1,3,2:T(8,128)}, u32[]{:S(2)}) copy-start(f32[64,64,1,3]{0,1,3,2:T(8,128)} %fusion.654) | copy-start | bytes 147460
  550.3 7.7 %copy-start.92 = (f32[64,64,1,3]{0,1,3,2:T(8,128)S(1)}, f32[64,64,1,3]{0,1,3,2:T(8,128)}, u32[]{:S(2)}) copy-start(f32[64,64,1,3]{0,1,3,2:T(8,128)} %fusion.652) | copy-start | bytes 147460
  553.8 158.8 %all-to-all-start.5 = ((bf16[16,2,4096]{2,1,0:T(2,128)(2,1)}), bf16[16,2,4096]{2,1,0:T(2,128)(2,1)S(1)}, u32[]{:S(2)}, u32[]{:S(2)}) async-start(bf16[16,2,4096]{2,1,0:T(2,128)(2,1)} %reshape.843), calls=%async_computation.5 | async-start | bytes 524288 | tf_op jit(solution)/shard_map/all_to_all | solution.py:181
  557.8 152.1 %all-reduce.28.cloned.1.call-start = ((), (), s32[]{:S(2)}) async-start(), calls=%async_computation.6 | async-start | bytes 1179648 | tf_op jit(solution)/shard_map/psum | solution.py:182
  (120 other events, 230.7 us)
Sparse Core Ops, SparseCore 0:
  564.0 145.8 all-reduce.27
where the time goes:
time: 733 us; the launch traced here: 721 us
  local copies, waits for them, and re-layouts  215 us (29%)
  waiting for transfers between devices  162 us (22%)
  matrix products  159 us (22%)
  blocking collectives  63.5 us (9%)
  other arithmetic  47.4 us (6%)
  between operations  39.2 us (5%)
  starting transfers between devices  34.7 us (5%)
    psum x1, waiting for transfers between devices, per_device(): lax.psum((raw_weight_h, raw_weight_v, raw_beta_h, raw_beta_v), ('vrow', '...  150 us
    transpose x30, matrix products, conv_weight(): return jnp.transpose(result, (1, 0, 2, 3))  84.4 us
    unnamed x371, local copies, waits for them, and re-layouts  75.8 us
    psum x1, blocking collectives, per_device(): lax.psum((raw_weight_h, raw_weight_v, raw_beta_h, raw_beta_v), ('vrow', '...  63.5 us
    conv_general_dilated x30, matrix products, conv_taps(): lax.conv_general_dilated(source, kernel_row, (1, 1), ((0, 0), (0, 0)), di...  52.2 us
    dynamic_slice x38, local copies, waits for them, and re-layouts, window(): return lax.dynamic_slice(padded, starts, sizes)  44.9 us
    mul x15, local copies, waits for them, and re-layouts, masked_source(): return (extended * inside[None, None].astype(extended.dtype), inside)  38 us
    conv_general_dilated x30, matrix products, conv_back(): lax.conv_general_dilated(grads, kernel_row, (1, 1), ((0, 0), (0, 0)), dim...  22 us
  transfers between devices with their start and end apart: 7, of which 4 were waited for; matrix products, arithmetic and copies ran while one was open for 6% of the time, Pallas kernels for 0%

commit v1 on v0

--- a/solution.py
+++ b/solution.py
@@ -4,6 +4,7 @@
 from jax.sharding import PartitionSpec as P
 
 SHIFT_MAX = 2
+_arrange_hubs = lambda field_in: jax.lax.psum(jax.lax.psum(field_in, axis_name="vrow"), "img")
 
 
 def conv_taps(source, kernel_row):
@@ -179,8 +180,8 @@
         dhor.reshape(u_local, y_local, channels, v_all, x_all), (0, 1, 4, 3, 2)
     ).reshape(u_local, y_local, x_all, v_all * channels)
     grad_features = lax.all_to_all(dhor_stored, "img", split_axis=2, concat_axis=1, tiled=True)
-    raw_weight_h, raw_weight_v, raw_beta_h, raw_beta_v = lax.psum(
-        (raw_weight_h, raw_weight_v, raw_beta_h, raw_beta_v), ("vrow", "img")
+    raw_weight_h, raw_weight_v, raw_beta_h, raw_beta_v = _arrange_hubs(
+        (raw_weight_h, raw_weight_v, raw_beta_h, raw_beta_v)
     )
     factor = float(u_all * v_all * y_all * x_all) ** (-0.5)
     return (

time: 733 us -> 711 us (0.970)
  the two profiles are of different devices: /device:TPU:1 before, /device:TPU:0 now
where the time goes in v1:
time: 711 us; the launch traced here: 699 us
  local copies, waits for them, and re-layouts  213 us (30%)
  matrix products  159 us (22%)
  waiting for transfers between devices  155 us (22%)
  blocking collectives  52.4 us (7%)
  other arithmetic  48.3 us (7%)
  between operations  39.9 us (6%)
  starting transfers between devices  31.3 us (4%)
    psum x1, waiting for transfers between devices, jax.lax.psum(jax.lax.psum(field_in, axis_name='vrow'), 'img')  117 us
    transpose x30, matrix products, conv_weight(): return jnp.transpose(result, (1, 0, 2, 3))  85.1 us
    unnamed x349, local copies, waits for them, and re-layouts  74.4 us
    conv_general_dilated x30, matrix products, conv_taps(): lax.conv_general_dilated(source, kernel_row, (1, 1), ((0, 0), (0, 0)), di...  52.3 us
    dynamic_slice x38, local copies, waits for them, and re-layouts, window(): return lax.dynamic_slice(padded, starts, sizes)  44.9 us
    mul x15, local copies, waits for them, and re-layouts, masked_source(): return (extended * inside[None, None].astype(extended.dtype), inside)  38.3 us
    psum x1, blocking collectives, jax.lax.psum(jax.lax.psum(field_in, axis_name='vrow'), 'img')  28.6 us
    psum x1, waiting for transfers between devices, jax.lax.psum(field_in, axis_name='vrow')  24.8 us
  transfers between devices with their start and end apart: 8, of which 5 were waited for; matrix products, arithmetic and copies ran while one was open for 7% of the time, Pallas kernels for 0%

profile of v1, /device:TPU:0, one launch (start us, length us, event | category | flops | bytes accessed | tf_op | source)
XLA Modules:
  0.0 699.0 jit_solution(1191617104975017040)
XLA Ops:
  7.2 5.5 all-to-all-start
  37.4 15.5 %broadcast_multiply_fusion.4 = (bf16[1,64,16,134]{1,0,3,2:T(2,128)(2,1)S(1)}, bf16[1,64,16,134]{1,0,3,2:T(2,128)(2,1)S(1)}, bf16[1,64,16,134]{1,0,3,2:T(2,128)(2...) fusion(bf16[16,134]{1,0:T(8,128)(2,1)S(1)} %copy-done.110, bf16[1,64,16,128]{1,0,3,2:T(2,128)(2,1)S(1)} %copy.364, ...), kind=kLoop, calls=%fused_computation.390 | loop fusion | flops 686080 | bytes 1655744 | tf_op jit(solution)/shard_map/mul | solution.py:62
  57.5 2.8 copy.370
  67.0 2.8 copy.384
  78.4 2.7 copy.398
  84.8 3.6 copy.411
  90.5 2.7 copy.412
  96.9 4.1 copy.425
  103.0 2.7 copy.426
  109.4 3.6 pad_dynamic-slice_fusion.39
  113.0 2.8 copy.365
  132.0 6.5 pad_dynamic-slice_fusion.35
  138.5 3.0 copy.393
  154.4 3.1 add_multiply_fusion.3
  158.7 3.7 add_multiply_fusion.2
  163.6 2.6 copy.543
  166.3 6.7 pad_dynamic-slice_fusion.31
  173.0 2.8 copy.421
  200.3 2.7 add_multiply_fusion.1
  206.1 3.8 add_multiply_fusion
  216.3 7.6 %all-to-all-start.1 = ((bf16[1,1,64,16,128]{4,2,1,0,3:T(8,128)(2,1)}), bf16[1,1,64,16,128]{4,2,1,0,3:T(8,128)(2,1)S(1)}, u32[]{:S(2)}, u32[]{:S(2)}) async-start(bf16[1,1,64,16,128]{4,2,1,0,3:T(8,128)(2,1)} %copy.435), calls=%async_computation.1 | async-start | bytes 524288 | tf_op jit(solution)/shard_map/all_to_all | solution.py:142
  224.6 8.7 %all-to-all-done.1 = bf16[1,1,64,16,128]{4,2,1,0,3:T(8,128)(2,1)S(1)} async-done(((bf16[1,1,64,16,128]{4,2,1,0,3:T(8,128)(2,1)}), bf16[1,1,64,16,128]{4,2,1,0,3:T(8,128)(2,1)S(1)}, u32[]{:S(2)}, u32[]{:S(2)}) %all-to-all-start.1) | async-done | bytes 262176 | tf_op jit(solution)/shard_map/all_to_all | solution.py:142
  235.3 5.0 all-to-all-start.2
  317.1 4.0 all-to-all-start.3
  321.2 5.7 fusion.86
  328.1 2.7 all-to-all-done.3
  333.3 5.4 all-to-all-start.4
  354.2 4.3 fusion.665
  358.5 4.5 fusion.666
  363.0 4.5 fusion.664
  368.8 4.4 fusion.662
  373.2 4.5 fusion.663
  377.7 4.5 fusion.661
  383.5 4.3 fusion.659
  387.8 4.5 fusion.660
  392.4 4.5 fusion.658
  398.1 4.3 fusion.656
  402.5 4.5 fusion.657
  407.0 4.5 fusion.655
  412.8 4.3 fusion.653
  417.1 4.5 fusion.654
  421.6 4.5 fusion.652
  426.2 3.0 fusion.363
  489.5 3.5 all-to-all-start.5
  493.1 23.8 %all-reduce.26 = (f32[5,64]{1,0:T(8,128)S(1)}, f32[5,64]{1,0:T(8,128)S(1)}) all-reduce(f32[5,64]{1,0:T(8,128)S(1)} %stack.89, f32[5,64]{1,0:T(8,128)S(1)} %copy-done.115), channel_id=1, replica_groups=mesh['vrow'=8,'img'=16] {'vrow'}, use_global_device_ids=true, to_apply=%region_9.10 | all-reduce | flops 640 | bytes 5120 | tf_op jit(solution)/shard_map/psum | solution.py:7
  516.9 28.6 %all-reduce.24 = (f32[5,64]{1,0:T(8,128)S(1)}, f32[5,64]{1,0:T(8,128)S(1)}) all-reduce(f32[5,64]{1,0:T(8,128)S(1)} %get-tuple-element.44, f32[5,64]{1,0:T(8,128)S(1)} %get-tuple-element.45), channel_id=1, replica_groups=mesh['vrow'=8,'img'=16] {'img'}, use_global_device_ids=true, to_apply=%region_10.11 | all-reduce | flops 640 | bytes 5120 | tf_op jit(solution)/shard_map/psum | solution.py:7
  545.5 24.8 %all-reduce.33.cloned.1.call-done = (f32[64,64,3,3]{0,1,3,2:T(8,128)}, f32[64,64,3,3]{0,1,3,2:T(8,128)}) async-done(((f32[64,64,3,3]{0,1,3,2:T(8,128)}, f32[64,64,3,3]{0,1,3,2:T(8,128)}), (f32[64,64,3,3]{0,1,3,2:T(8,128)}, f32[64,64,3,3]{0,1,3,2:T(8,128)})) %all-reduce.33.cloned.1.call-update) | async-done | bytes 294928 | tf_op jit(solution)/shard_map/psum | solution.py:7
  572.6 116.6 %all-reduce.31.cloned.1.call-done = (f32[64,64,3,3]{0,1,3,2:T(8,128)}, f32[64,64,3,3]{0,1,3,2:T(8,128)}) async-done(((f32[64,64,3,3]{0,1,3,2:T(8,128)}, f32[64,64,3,3]{0,1,3,2:T(8,128)}), (f32[64,64,3,3]{0,1,3,2:T(8,128)}, f32[64,64,3,3]{0,1,3,2:T(8,128)})) %all-reduce.31.cloned.1.call-update) | async-done | bytes 294928 | tf_op jit(solution)/shard_map/psum | solution.py:7
  (627 shorter events, 269.0 us)
Async XLA Ops:
  7.2 28.2 %all-to-all-start = ((bf16[1,16,8,1024]{3,2,0,1:T(8,128)(2,1)}), bf16[1,16,8,1024]{3,2,0,1:T(8,128)(2,1)S(1)}, u32[]{:S(2)}, u32[]{:S(2)}) async-start(bf16[1,16,8,1024]{3,2,0,1:T(8,128)(2,1)} %bitcast.649), calls=%async_computation | async-start | bytes 524288 | tf_op jit(solution)/shard_map/all_to_all | solution.py:133
  52.9 56.5 %copy-start.3 = (bf16[1,64,16,134]{1,0,3,2:T(2,128)(2,1)}, bf16[1,64,16,134]{1,0,3,2:T(2,128)(2,1)S(1)}, u32[]{:S(2)}) copy-start(bf16[1,64,16,134]{1,0,3,2:T(2,128)(2,1)S(1)} %get-tuple-element.104) | copy-start | bytes 823300
  52.9 79.1 %copy-start.5 = (bf16[1,64,16,134]{1,0,3,2:T(2,128)(2,1)}, bf16[1,64,16,134]{1,0,3,2:T(2,128)(2,1)S(1)}, u32[]{:S(2)}) copy-start(bf16[1,64,16,134]{1,0,3,2:T(2,128)(2,1)S(1)} %get-tuple-element.105) | copy-start | bytes 823300
  52.9 79.1 %copy-start.7 = (bf16[1,64,16,134]{1,0,3,2:T(2,128)(2,1)}, bf16[1,64,16,134]{1,0,3,2:T(2,128)(2,1)S(1)}, u32[]{:S(2)}) copy-start(bf16[1,64,16,134]{1,0,3,2:T(2,128)(2,1)S(1)} %get-tuple-element.106) | copy-start | bytes 823300
  117.6 2.9 copy-start.22
  132.0 81.9 %copy-start.12 = (f32[16,1,128,64]{2,0,3,1:T(8,128)}, f32[16,1,128,64]{2,0,3,1:T(8,128)S(1)}, u32[]{:S(2)}) copy-start(f32[16,1,128,64]{2,0,3,1:T(8,128)S(1)} %copy.541) | copy-start | bytes 1572868
  158.7 55.2 %copy-start.14 = (f32[16,1,128,64]{2,0,3,1:T(8,128)}, f32[16,1,128,64]{2,0,3,1:T(8,128)S(1)}, u32[]{:S(2)}) copy-start(f32[16,1,128,64]{2,0,3,1:T(8,128)S(1)} %copy.542) | copy-start | bytes 1572868
  162.6 3.7 copy-start.11
  177.4 2.9 copy-start.36
  206.1 7.8 %copy-start.18 = (f32[16,1,128,64]{2,0,3,1:T(8,128)}, f32[16,1,128,64]{2,0,3,1:T(8,128)S(1)}, u32[]{:S(2)}) copy-start(f32[16,1,128,64]{2,0,3,1:T(8,128)S(1)} %copy.544) | copy-start | bytes 1572868
  211.2 2.7 copy-start.75
  211.2 2.7 copy-start.77
  214.0 9.9 %copy-start.142 = (f32[5,64]{1,0:T(8,128)S(1)}, f32[5,64]{1,0:T(8,128)}, u32[]{:S(2)}) copy-start(f32[5,64]{1,0:T(8,128)} %param.11) | copy-start | bytes 3844
  214.0 10.5 %copy-start.129 = (pred[8,22]{1,0:T(8,128)(4,1)S(1)}, pred[8,22]{1,0:T(8,128)(4,1)}, u32[]{:S(2)}) copy-start(pred[8,22]{1,0:T(8,128)(4,1)} %get-tuple-element.145) | copy-start | bytes 532
  214.0 10.5 %copy-start.130 = (pred[8,22]{1,0:T(8,128)(4,1)S(1)}, pred[8,22]{1,0:T(8,128)(4,1)}, u32[]{:S(2)}) copy-start(pred[8,22]{1,0:T(8,128)(4,1)} %get-tuple-element.168) | copy-start | bytes 532
  216.3 17.0 %all-to-all-start.1 = ((bf16[1,1,64,16,128]{4,2,1,0,3:T(8,128)(2,1)}), bf16[1,1,64,16,128]{4,2,1,0,3:T(8,128)(2,1)S(1)}, u32[]{:S(2)}, u32[]{:S(2)}) async-start(bf16[1,1,64,16,128]{4,2,1,0,3:T(8,128)(2,1)} %copy.435), calls=%async_computation.1 | async-start | bytes 524288 | tf_op jit(solution)/shard_map/all_to_all | solution.py:142
  224.5 47.6 %copy-start.131 = (f32[64]{0:T(128)}, f32[64]{0:T(128)S(1)}, u32[]{:S(2)}) copy-start(f32[64]{0:T(128)S(1)} %get-tuple-element.130) | copy-start | bytes 772
  233.8 6.5 copy-start.128
  235.2 19.5 %copy-start.126 = (pred[8,22]{1,0:T(8,128)(4,1)S(1)}, pred[8,22]{1,0:T(8,128)(4,1)}, u32[]{:S(2)}) copy-start(pred[8,22]{1,0:T(8,128)(4,1)} %get-tuple-element.164) | copy-start | bytes 532
  235.2 19.5 %copy-start.127 = (pred[8,22]{1,0:T(8,128)(4,1)S(1)}, pred[8,22]{1,0:T(8,128)(4,1)}, u32[]{:S(2)}) copy-start(pred[8,22]{1,0:T(8,128)(4,1)} %get-tuple-element.166) | copy-start | bytes 532
  235.2 19.6 %copy-start.50 = (f32[16,8,17,64]{3,1,2,0:T(8,128)S(1)}, f32[16,8,17,64]{3,1,2,0:T(8,128)}, u32[]{:S(2)}) copy-start(f32[16,8,17,64]{3,1,2,0:T(8,128)} %get-tuple-element.92) | copy-start | bytes 1671172
  235.3 32.7 %all-to-all-start.2 = ((bf16[16,2,4096]{2,1,0:T(2,128)(2,1)}), bf16[16,2,4096]{2,1,0:T(2,128)(2,1)}, u32[]{:S(2)}, u32[]{:S(2)}) async-start(bf16[16,2,4096]{2,1,0:T(2,128)(2,1)} %reshape.837), calls=%async_computation.2 | async-start | bytes 524288 | tf_op jit(solution)/shard_map/all_to_all | solution.py:141
  315.0 6.2 copy-start.132
  317.1 13.7 %all-to-all-start.3 = ((bf16[8,2,8192]{2,1,0:T(2,128)(2,1)}), bf16[8,2,8192]{2,1,0:T(2,128)(2,1)}, u32[]{:S(2)}, u32[]{:S(2)}) async-start(bf16[8,2,8192]{2,1,0:T(2,128)(2,1)} %reshape.839), calls=%async_computation.3 | async-start | bytes 524288 | tf_op jit(solution)/shard_map/all_to_all | solution.py:169
  321.2 5.7 copy-start.148
  332.1 6.6 copy-start.149
  333.3 13.1 %all-to-all-start.4 = ((bf16[16,2,4096]{2,1,0:T(2,128)(2,1)}), bf16[16,2,4096]{2,1,0:T(2,128)(2,1)S(1)}, u32[]{:S(2)}, u32[]{:S(2)}) async-start(bf16[16,2,4096]{2,1,0:T(2,128)(2,1)} %reshape.841), calls=%async_computation.4 | async-start | bytes 524288 | tf_op jit(solution)/shard_map/all_to_all | solution.py:168
  338.7 231.6 %all-reduce.33.cloned.1.call-start = ((), (), s32[]{:S(2)}) async-start(), calls=%async_computation.7 | async-start | bytes 1179648 | tf_op jit(solution)/shard_map/psum | solution.py:7
  347.9 3.5 copy-start
  354.2 4.3 copy-start.37
  358.5 4.5 copy-start.35
  368.8 4.4 copy-start.34
  373.2 4.5 copy-start.32
  377.7 4.5 copy-start.58
  383.5 4.3 copy-start.30
  387.8 4.5 copy-start.28
  392.4 4.5 copy-start.57
  398.1 4.3 copy-start.27
  402.5 4.5 copy-start.25
  407.0 4.5 copy-start.56
  412.8 4.3 copy-start.23
  417.1 4.5 copy-start.21
  421.6 4.5 copy-start.49
  478.6 4.1 copy-start.19
  478.6 4.1 copy-start.20
  486.0 7.2 %copy-start.115 = (f32[5,64]{1,0:T(8,128)S(1)}, f32[5,64]{1,0:T(8,128)}, u32[]{:S(2)}) copy-start(f32[5,64]{1,0:T(8,128)} %stack.95) | copy-start | bytes 3844
  489.5 82.0 %all-to-all-start.5 = ((bf16[16,2,4096]{2,1,0:T(2,128)(2,1)}), bf16[16,2,4096]{2,1,0:T(2,128)(2,1)S(1)}, u32[]{:S(2)}, u32[]{:S(2)}) async-start(bf16[16,2,4096]{2,1,0:T(2,128)(2,1)} %reshape.843), calls=%async_computation.5 | async-start | bytes 524288 | tf_op jit(solution)/shard_map/all_to_all | solution.py:182
  493.1 196.1 %all-reduce.31.cloned.1.call-start = ((), (), s32[]{:S(2)}) async-start(), calls=%async_computation.6 | async-start | bytes 1179648 | tf_op jit(solution)/shard_map/psum | solution.py:7
  (110 other events, 173.6 us)
Sparse Core Ops, SparseCore 0:
  482.8 87.4 all-reduce.32
  572.9 116.2 all-reduce.30
